TPU v7x, 256 devices: a whole 4x4x8 slice. The times are simulated.
256 devices in a mesh: dp: 8 (over x, core), grid: 32 (over y, z).
Axes of the slice: x: 4, y: 4, z: 8, core: 2. Of those that a mesh axis runs over, the one named last changes fastest.
Arguments:
- q_row: bfloat16 [16, 96, 96, 1536], P('dp', 'grid'), may hold values from -8 to 8, as said below
- k_row: bfloat16 [16, 96, 96, 1536], P('dp', 'grid'), may hold values from -8 to 8
- v_row: bfloat16 [16, 96, 96, 1536], P('dp', 'grid'), may hold values from -6 to 6
- q_col: bfloat16 [16, 96, 96, 1536], P('dp', None, 'grid'), may hold values from -8 to 8, as said below
- k_col: bfloat16 [16, 96, 96, 1536], P('dp', None, 'grid'), may hold values from -8 to 8
- cotangent: bfloat16 [16, 96, 96, 1536], P('dp', None, 'grid'), may hold values from -6 to 6
- w_value: bfloat16 [1536, 1536], P(('dp', 'grid')), may hold values from -0.15625 to 0.15625
- row_positions: int32 [96], replicated, may hold values from 0 to 95, each once
- col_positions: int32 [96], replicated, may hold values from 0 to 95, each once
- mlp_in: float32 [512], P('grid'), may hold values from -8 to 8
- mlp_bias: float32 [512], P('grid'), may hold values from -4 to 4
- mlp_out: float32 [512, 48], P('grid'), may hold values from -0.08 to 0.08
Outputs:
- attended: bfloat16 [16, 96, 96, 1536], P('dp', None, 'grid')
- grad_mlp_in: float32 [512], P('grid')
- grad_mlp_bias: float32 [512], P('grid')
- grad_mlp_out: float32 [512, 48], P('grid')
Inputs may be any that keep to these rules, and one draw needn't show every extreme that they name: q_row and k_row lie within the range. q_col and k_col lie within the range. `row_positions`: each of 0 to 95 appears once. `col_positions`: each of 0 to 95 appears once.
All inputs are finite; a program needn't handle non-finite values.
Results may differ from a plain program's by a relative error of at most 0.007.
Values may be sent and summed in bfloat16 or wider, within the bound.
No kernel may reach another device: no remote copies, remote signals or barrier semaphores. Data moves between devices by JAX's collectives and lax.ppermute only.
A program may use at most 192 MiB of HBM per device.

v0:
```python
import jax
import jax.numpy as jnp
from jax import lax
from jax.sharding import PartitionSpec as P

G = 96
D = 1536
NH = 48
HD = 32
NOFF = 191
PRECISE = lax.Precision.HIGHEST


def offset_coords():
    delta = jnp.arange(NOFF, dtype=jnp.float32) - (G - 1)
    scaled = delta * (8.0 / (G - 1))
    return jnp.sign(scaled) * jnp.log2(jnp.abs(scaled) + 1.0) / 3.0


def offset_one_hot(positions):
    spread = positions[:, None] - positions[None, :] + (G - 1)
    levels = jnp.arange(NOFF, dtype=jnp.int32)
    return (spread.reshape(-1)[:, None] == levels[None, :]).astype(jnp.float32)


def expand_bias(one_hot, bias_table):
    flat_bias = jnp.dot(one_hot, bias_table, precision=PRECISE)
    return flat_bias.reshape(G, G, NH).transpose(2, 0, 1)


def fold_bias(one_hot, bias_grad):
    flat_grad = bias_grad.transpose(1, 2, 0).reshape(G * G, NH)
    return lax.dot_general(one_hot, flat_grad, (((0,), (0,)), ((), ())), precision=PRECISE)


def soft_grad(attn_probs, d_probs):
    return attn_probs * (d_probs - jnp.sum(attn_probs * d_probs, axis=-1, keepdims=True))


def fetch_weight(w_value):
    return lax.all_gather(w_value, ("dp", "grid"), axis=0, tiled=True)


def shards(
    q_row,
    k_row,
    v_row,
    q_col,
    k_col,
    cotangent,
    w_value,
    row_positions,
    col_positions,
    mlp_in,
    mlp_bias,
    mlp_out,
):
    images = q_row.shape[0]
    row_count = q_row.shape[1]
    col_count = q_col.shape[2]
    coords = offset_coords()
    pre_act = coords[:, None] * mlp_in[None, :] + mlp_bias[None, :]
    hidden_units = jnp.maximum(pre_act, 0.0)
    partial_table = jnp.dot(hidden_units, mlp_out, precision=PRECISE)
    table_pre = lax.psum(partial_table, "grid")
    squashed = jax.nn.sigmoid(table_pre)
    bias_table = 16.0 * squashed
    hot_cols = offset_one_hot(col_positions)
    hot_rows = offset_one_hot(row_positions)
    bias_row = expand_bias(hot_cols, bias_table)
    bias_col = expand_bias(hot_rows, bias_table)
    score_scale = HD ** (-0.5)
    query_rows = q_row.reshape(images * row_count, G, NH, HD)
    key_rows = k_row.reshape(images * row_count, G, NH, HD)
    value_rows = v_row.reshape(images * row_count, G, NH, HD)
    scores = (
        jnp.einsum("nqhd,nkhd->nhqk", query_rows, key_rows, preferred_element_type=jnp.float32)
        * score_scale
        + bias_row[None]
    )
    p_row = jax.nn.softmax(scores, axis=-1)
    p_row_b = p_row.astype(jnp.bfloat16)
    row_out = jnp.einsum(
        "nhqk,nkhd->nqhd", p_row_b, value_rows, preferred_element_type=jnp.float32
    ).astype(jnp.bfloat16)
    flat_out = row_out.reshape(images * row_count * G, D)
    whole_weight = fetch_weight(w_value)
    projected = jnp.dot(flat_out, whole_weight, preferred_element_type=jnp.float32)
    values = projected.astype(jnp.bfloat16).reshape(images, row_count, G, D)
    col_values = lax.all_to_all(values, "grid", split_axis=2, concat_axis=1, tiled=True)
    query_cols = q_col.reshape(images, G, col_count, NH, HD)
    key_cols = k_col.reshape(images, G, col_count, NH, HD)
    value_cols = col_values.reshape(images, G, col_count, NH, HD)
    scores_col = (
        jnp.einsum("bqchd,bkchd->bchqk", query_cols, key_cols, preferred_element_type=jnp.float32)
        * score_scale
        + bias_col
    )
    p_col = jax.nn.softmax(scores_col, axis=-1)
    p_col_b = p_col.astype(jnp.bfloat16)
    attended = (
        jnp.einsum("bchqk,bkchd->bqchd", p_col_b, value_cols, preferred_element_type=jnp.float32)
        .astype(jnp.bfloat16)
        .reshape(images, G, col_count, D)
    )
    grad_cols = cotangent.reshape(images, G, col_count, NH, HD)
    dprob_col = jnp.einsum(
        "bqchd,bkchd->bchqk", grad_cols, value_cols, preferred_element_type=jnp.float32
    )
    ds_col = soft_grad(p_col, dprob_col)
    col_table = fold_bias(hot_rows, jnp.sum(ds_col, axis=(0, 1)))
    col_summed = lax.psum(col_table, ("dp", "grid"))
    d_values = (
        jnp.einsum("bchqk,bqchd->bkchd", p_col_b, grad_cols, preferred_element_type=jnp.float32)
        .astype(jnp.bfloat16)
        .reshape(images, G, col_count, D)
    )
    d_rows = lax.all_to_all(d_values, "grid", split_axis=1, concat_axis=2, tiled=True)
    flat_grad = d_rows.reshape(images * row_count * G, D)
    d_flat = lax.dot_general(
        flat_grad, whole_weight, (((1,), (1,)), ((), ())), preferred_element_type=jnp.float32
    )
    d_row_out = d_flat.astype(jnp.bfloat16).reshape(images * row_count, G, NH, HD)
    dprob_row = jnp.einsum(
        "nqhd,nkhd->nhqk", d_row_out, value_rows, preferred_element_type=jnp.float32
    )
    ds_row = soft_grad(p_row, dprob_row)
    row_table = fold_bias(hot_cols, jnp.sum(ds_row, axis=0))
    table_sum = col_summed + lax.psum(row_table, ("dp", "grid"))
    batch_size = lax.axis_size("dp") * images
    table_grad = table_sum / (batch_size * G)
    pre_grad = table_grad * 16.0 * squashed * (1.0 - squashed)
    grad_mlp_out = lax.dot_general(
        hidden_units, pre_grad, (((0,), (0,)), ((), ())), precision=PRECISE
    )
    back_units = lax.dot_general(pre_grad, mlp_out, (((1,), (1,)), ((), ())), precision=PRECISE)
    unit_grad = jnp.where(pre_act > 0, back_units, 0.0)
    grad_mlp_in = jnp.sum(unit_grad * coords[:, None], axis=0)
    grad_mlp_bias = jnp.sum(unit_grad, axis=0)
    return (attended, grad_mlp_in, grad_mlp_bias, grad_mlp_out)


def solution(mesh):
    return jax.shard_map(
        shards,
        mesh=mesh,
        in_specs=(
            P("dp", "grid", None, None),
            P("dp", "grid", None, None),
            P("dp", "grid", None, None),
            P("dp", None, "grid", None),
            P("dp", None, "grid", None),
            P("dp", None, "grid", None),
            P(("dp", "grid"), None),
            P(),
            P(),
            P("grid"),
            P("grid"),
            P("grid", None),
        ),
        out_specs=(P("dp", None, "grid", None), P("grid"), P("grid"), P("grid", None)),
        check_vma=False,
    )
```

profile of v0, /device:TPU:1, one launch (start us, length us, event | category | flops | bytes accessed | tf_op | source)
XLA Modules:
  0.0 479.7 jit_solution(3552161299242555741)
XLA Ops:
  10.4 119.0 %psum.21 = f32[191,48]{0,1:T(8,128)S(1)} all-reduce(f32[191,48]{0,1:T(8,128)S(1)} %fusion.55), channel_id=1, replica_groups=mesh['dp'=8,'grid'=32] {'grid'}, use_global_device_ids=true, to_apply=%region_0.0 | all-reduce | flops 9168 | bytes 73344 | tf_op jit(solution)/shard_map/psum | solution.py:65
  129.4 4.4 fusion.11
  147.5 11.3 %fusion.79 = (f32[2,3,48,96]{3,2,1,0:T(8,128)S(1)}, f32[2,3,48,96,96]{3,4,2,1,0:T(8,128)}) fusion(f32[48,96,96]{1,2,0:T(8,128)} %bitcast.78, bf16[2,96,3,48,32]{1,4,3,2,0:T(8,128)(2,1)} %bitcast.86, bf16[2,96,3,48,32]{1,4,3,2,0:T(8,128)(2,1)} %bitcast.87), kind=kOutput, calls=%fused_computation.87 | convolution fusion | flops 180486240 | bytes 16035840 | tf_op jit(solution)/shard_map/sub | solution.py:99
  158.8 10.2 %fusion.35 = bf16[2,3,48,96,32]{3,4,2,1,0:T(8,128)(2,1)} fusion(bf16[2,96,3,48,32]{1,4,3,2,0:T(8,128)(2,1)S(1)} %bitcast.75, f32[2,3,48,96,96]{3,4,2,1,0:T(8,128)} %get-tuple-element.33, f32[2,3,48,96]{3,2,1,0:T(8,128)S(1)} %get-tuple-element.32), kind=kOutput, calls=%fused_computation.47 | convolution fusion | flops 176062464 | bytes 14266368 | tf_op jit(solution)/shard_map/bchqk,bqchd->bkchd/dot_general | solution.py:114
  169.1 5.3 %copy.141 = bf16[2,96,3,1536]{3,0,2,1:T(2,128)(2,1)} copy(bf16[2,96,3,1536]{1,3,2,0:T(8,128)(2,1)} %bitcast.90) | data formatting | bytes 3538944 | tf_op jit(solution)/shard_map/reshape | solution.py:116
  174.4 5.0 %all-to-all-start.1 = ((bf16[2,96,3,1536]{3,0,2,1:T(2,128)(2,1)}), bf16[2,96,3,1536]{3,0,2,1:T(2,128)(2,1)}, u32[]{:S(2)}, u32[]{:S(2)}) async-start(bf16[2,96,3,1536]{3,0,2,1:T(2,128)(2,1)} %copy.141), calls=%async_computation.1 | async-start | bytes 3538944 | tf_op jit(solution)/shard_map/all_to_all | solution.py:118
  179.6 4.5 fusion.17
  194.8 4.2 copy.126
  198.9 11.3 %fusion.78 = (f32[6,48,96]{2,1,0:T(8,128)S(1)}, f32[6,48,96,96]{2,3,1,0:T(8,128)}) fusion(f32[48,96,96]{1,2,0:T(8,128)S(1)} %bitcast.79, bf16[6,96,48,32]{1,3,2,0:T(8,128)(2,1)} %bitcast.88, bf16[6,96,48,32]{1,3,2,0:T(8,128)(2,1)} %bitcast.89), kind=kOutput, calls=%fused_computation.86 | convolution fusion | flops 180486240 | bytes 16035840 | tf_op jit(solution)/shard_map/sub | solution.py:81
  210.2 7.7 %convert_bitcast_fusion = bf16[6,96,48,32]{1,3,2,0:T(8,128)(2,1)S(1)} fusion(bf16[6,96,48,32]{1,3,2,0:T(8,128)(2,1)} %bitcast.82, f32[6,48,96,96]{2,3,1,0:T(8,128)} %get-tuple-element.31, f32[6,48,96]{2,1,0:T(8,128)S(1)} %get-tuple-element.30), kind=kOutput, calls=%fused_computation.44 | convolution fusion | flops 176062464 | bytes 14266368 | tf_op jit(solution)/shard_map/nhqk,nkhd->nqhd/dot_general | solution.py:83
  229.5 8.5 %reshape.139 = bf16[1536,1536]{1,0:T(8,128)(2,1)} reshape(bf16[256,6,1536]{2,1,0:T(8,128)(2,1)} %all-gather.3.cloned.1.call-done) | data formatting | bytes 9437184
  238.0 6.4 %convolution_convert_fusion.1 = bf16[576,1536]{1,0:T(8,128)(2,1)} fusion(bf16[576,1536]{1,0:T(8,128)(2,1)S(1)} %copy-done.9, bf16[1536,1536]{1,0:T(8,128)(2,1)} %reshape.139), kind=kOutput, calls=%fused_computation.41 | convolution fusion | flops 2718793728 | bytes 8257536 | tf_op jit(solution)/shard_map/dot_general | solution.py:120
  250.8 5.9 %convolution_convert_fusion = bf16[576,1536]{1,0:T(8,128)(2,1)S(1)} fusion(bf16[576,1536]{0,1:T(8,128)(2,1)} %reshape.125, bf16[1536,1536]{1,0:T(8,128)(2,1)} %reshape.139), kind=kOutput, calls=%fused_computation.40 | convolution fusion | flops 2718793728 | bytes 8257536 | tf_op jit(solution)/shard_map/dot_general | solution.py:88
  259.7 10.2 %all-to-all-start = ((bf16[2,3,96,1536]{3,0,1,2:T(2,128)(2,1)}), bf16[2,3,96,1536]{3,0,1,2:T(2,128)(2,1)}, u32[]{:S(2)}, u32[]{:S(2)}) async-start(bf16[2,3,96,1536]{3,0,1,2:T(2,128)(2,1)} %copy.129), calls=%async_computation | async-start | bytes 3538944 | tf_op jit(solution)/shard_map/all_to_all | solution.py:90
  269.9 10.4 %fusion = f32[6,48,96,96]{2,3,1,0:T(8,128)} fusion(bf16[6,96,48,32]{1,3,2,0:T(8,128)(2,1)} %bitcast.83, bf16[6,96,48,32]{1,0,3,2:T(8,128)(2,1)S(1)} %copy-done.4, f32[6,48,96,96]{2,3,1,0:T(8,128)} %get-tuple-element.31, f32[6,48,96]{2,1,0:T(8,128)S(1)} %get-tuple-element.30), kind=kOutput, calls=%fused_computation | convolution fusion | flops 175205472 | bytes 24883200 | tf_op jit(solution)/shard_map/sub | solution.py:37
  280.3 13.5 %multiply_reduce_fusion = f32[48,96,96]{1,2,0:T(8,128)} fusion(f32[6,48,96,96]{2,3,1,0:T(8,128)} %fusion, f32[6,48,96,96]{2,3,1,0:T(8,128)} %get-tuple-element.31, f32[6,48,96]{2,1,0:T(8,128)S(1)} %get-tuple-element.30, bf16[6,96,48,32]{1,3,2,0:T(8,128)(2,1)} %bitcast.84, bf16[6,96,48,32]{1,0,3,2:T(8,128)(2,1)S(1)} %copy-done.4), kind=kOutput, calls=%fused_computation.8 | convolution fusion | flops 180043776 | bytes 26652672 | tf_op jit(solution)/shard_map/nqhd,nkhd->nhqk/dot_general | solution.py:124
  301.0 6.1 %reshape.127 = bf16[2,96,3,48,32]{4,3,0,2,1:T(8,128)(2,1)} reshape(bf16[2,32,3,3,1536]{4,0,3,2,1:T(2,128)(2,1)S(1)} %copy.131) | data formatting | bytes 3538944 | tf_op jit(solution)/shard_map/reshape | solution.py:93
  307.2 8.3 %copy.135 = bf16[2,96,3,48,32]{1,4,3,2,0:T(8,128)(2,1)} copy(bf16[2,96,3,48,32]{4,3,0,2,1:T(8,128)(2,1)} %reshape.127) | data formatting | bytes 3538944 | tf_op jit(solution)/shard_map/reshape | solution.py:93
  315.5 9.4 %fusion.32 = bf16[2,3,48,32,96]{4,3,2,1,0:T(8,128)(2,1)} fusion(bf16[2,96,3,48,32]{1,4,3,2,0:T(8,128)(2,1)} %copy.135, f32[2,3,48,96,96]{3,4,2,1,0:T(8,128)} %get-tuple-element.33, f32[2,3,48,96]{3,2,1,0:T(8,128)S(1)} %get-tuple-element.32), kind=kOutput, calls=%fused_computation.46 | convolution fusion | flops 176062464 | bytes 14266368 | tf_op jit(solution)/shard_map/bchqk,bkchd->bqchd/dot_general | solution.py:102
  325.0 6.3 %fusion.80 = f32[2,3,48,96,96]{4,3,2,1,0:T(8,128)} fusion(bf16[2,96,3,48,32]{1,4,3,2,0:T(8,128)(2,1)S(1)} %copy-done.3, bf16[2,96,3,48,32]{1,4,3,2,0:T(8,128)(2,1)S(1)} %bitcast.76), kind=kOutput, calls=%fused_computation.88 | convolution fusion | flops 169869312 | bytes 14155776 | tf_op jit(solution)/shard_map/bqchd,bkchd->bchqk/dot_general | solution.py:107
  331.2 17.8 %fusion.5 = f32[48,96,96]{1,2,0:T(8,128)} fusion(f32[2,3,48,96,96]{4,3,2,1,0:T(8,128)} %fusion.80, f32[2,3,48,96,96]{3,4,2,1,0:T(8,128)} %get-tuple-element.33, f32[2,3,48,96]{3,2,1,0:T(8,128)S(1)} %get-tuple-element.32, bf16[2,96,3,48,32]{1,4,3,2,0:T(8,128)(2,1)} %copy.135, bf16[2,96,3,48,32]{1,4,3,2,0:T(8,128)(2,1)S(1)} %bitcast.77), kind=kOutput, calls=%fused_computation.7 | convolution fusion | flops 185379936 | bytes 26652672 | tf_op jit(solution)/shard_map/sub | solution.py:37
  353.6 5.4 %fusion.10 = f32[191,48]{0,1:T(8,128)S(1)} fusion(f32[9216,48]{0,1:T(8,128)} %reshape.133, s32[9216]{0:T(1024)S(1)} %copy-done.11), kind=kOutput, calls=%fused_computation.20 | convolution fusion | flops 1015667712 | bytes 1843008 | tf_op jit(solution)/shard_map/dot_general | solution.py:33
  359.0 5.3 %fusion.46 = f32[191,48]{0,1:T(8,128)S(1)} fusion(f32[191,48]{0,1:T(8,128)S(1)} %fusion.10, f32[9216,48]{0,1:T(8,128)} %reshape.137, s32[9216]{0:T(1024)S(1)} %add.74), kind=kOutput, calls=%fused_computation.49 | convolution fusion | flops 1015676864 | bytes 1879680 | tf_op jit(solution)/shard_map/dot_general | solution.py:33
  364.3 104.5 %psum.24 = f32[191,48]{0,1:T(8,128)S(1)} all-reduce(f32[191,48]{0,1:T(8,128)S(1)} %fusion.46), channel_id=1, replica_groups=mesh['dp'=8,'grid'=32] {'dp','grid'}, use_global_device_ids=true, to_apply=%region_7.0 | all-reduce | flops 9168 | bytes 73344 | tf_op jit(solution)/shard_map/psum | solution.py:112
  (69 shorter events, 64.3 us)
Async XLA Ops:
  7.2 2.3 copy-start
  7.2 222.3 %all-gather.3.cloned.1.call-start = ((), (), s32[]{:S(2)}) async-start(), calls=%async_computation.2 | async-start | bytes 6316032 | tf_op jit(solution)/shard_map/all_gather | solution.py:41
  8.8 120.6 %copy-start.10 = (s32[9216]{0:T(1024)}, s32[9216]{0:T(1024)S(1)}, u32[]{:S(2)}) copy-start(s32[9216]{0:T(1024)S(1)} %add.83) | copy-start | bytes 110596
  8.9 0.6 copy-start.15
  138.0 4.1 copy-start.7
  147.5 11.3 %copy-start.1 = (bf16[2,96,3,1536]{1,3,2,0:T(8,128)(2,1)}, bf16[2,96,3,1536]{1,3,2,0:T(8,128)(2,1)S(1)}, u32[]{:S(2)}) copy-start(bf16[2,96,3,1536]{1,3,2,0:T(8,128)(2,1)S(1)} %copy.137) | copy-start | bytes 5308420
  174.3 5.0 %copy-start.12 = (s32[96]{0:T(128)S(1)}, s32[96]{0:T(128)}, u32[]{:S(2)}) copy-start(s32[96]{0:T(128)} %param.20) | copy-start | bytes 1156
  174.4 49.6 %all-to-all-start.1 = ((bf16[2,96,3,1536]{3,0,2,1:T(2,128)(2,1)}), bf16[2,96,3,1536]{3,0,2,1:T(2,128)(2,1)}, u32[]{:S(2)}, u32[]{:S(2)}) async-start(bf16[2,96,3,1536]{3,0,2,1:T(2,128)(2,1)} %copy.141), calls=%async_computation.1 | async-start | bytes 3538944 | tf_op jit(solution)/shard_map/all_to_all | solution.py:118
  188.2 4.1 copy-start.8
  194.8 4.2 copy-start.5
  229.5 8.5 %copy-start.9 = (bf16[576,1536]{1,0:T(8,128)(2,1)S(1)}, bf16[576,1536]{1,0:T(8,128)(2,1)}, u32[]{:S(2)}) copy-start(bf16[576,1536]{1,0:T(8,128)(2,1)} %reshape.135) | copy-start | bytes 5308420
  259.7 10.2 %copy-start.4 = (bf16[6,96,48,32]{1,0,3,2:T(8,128)(2,1)S(1)}, bf16[6,96,48,32]{1,0,3,2:T(8,128)(2,1)}, u32[]{:S(2)}) copy-start(bf16[6,96,48,32]{1,0,3,2:T(8,128)(2,1)} %reshape.136) | copy-start | bytes 5308420
  259.7 38.7 %all-to-all-start = ((bf16[2,3,96,1536]{3,0,1,2:T(2,128)(2,1)}), bf16[2,3,96,1536]{3,0,1,2:T(2,128)(2,1)}, u32[]{:S(2)}, u32[]{:S(2)}) async-start(bf16[2,3,96,1536]{3,0,1,2:T(2,128)(2,1)} %copy.129), calls=%async_computation | async-start | bytes 3538944 | tf_op jit(solution)/shard_map/all_to_all | solution.py:90
  315.5 9.4 %copy-start.2 = (bf16[2,96,3,1536]{1,3,2,0:T(8,128)(2,1)S(1)}, bf16[2,96,3,1536]{1,3,2,0:T(8,128)(2,1)}, u32[]{:S(2)}) copy-start(bf16[2,96,3,1536]{1,3,2,0:T(8,128)(2,1)} %copy-done.1) | copy-start | bytes 5308420
  315.5 9.4 %copy-start.3 = (bf16[2,96,3,48,32]{1,4,3,2,0:T(8,128)(2,1)S(1)}, bf16[2,96,3,48,32]{1,4,3,2,0:T(8,128)(2,1)}, u32[]{:S(2)}) copy-start(bf16[2,96,3,48,32]{1,4,3,2,0:T(8,128)(2,1)} %copy.135) | copy-start | bytes 5308420
  351.0 2.5 copy-start.11
  353.6 115.2 %copy-start.13 = (f32[16]{0:T(128)S(1)}, f32[16]{0:T(128)}, u32[]{:S(2)}) copy-start(f32[16]{0:T(128)} %param.22) | copy-start | bytes 196
  353.6 115.2 %copy-start.14 = (f32[16]{0:T(128)S(1)}, f32[16]{0:T(128)}, u32[]{:S(2)}) copy-start(f32[16]{0:T(128)} %param.21) | copy-start | bytes 196
  353.6 115.2 %copy-start.16 = (f32[191]{0:T(256)S(1)}, f32[191]{0:T(256)}, u32[]{:S(2)}) copy-start(f32[191]{0:T(256)} %copy-done.15) | copy-start | bytes 2296
  353.6 116.8 %copy-start.6 = (bf16[2,3,48,32,96]{4,3,2,1,0:T(8,128)(2,1)S(1)}, bf16[2,3,48,32,96]{4,3,2,1,0:T(8,128)(2,1)}, u32[]{:S(2)}) copy-start(bf16[2,3,48,32,96]{4,3,2,1,0:T(8,128)(2,1)} %fusion.32) | copy-start | bytes 5308420
Sparse Core Ops, SparseCore 0:
  11.8 121.0 all-gather.2
where the time goes:
time: 489 us; the launch traced here: 480 us
  blocking collectives  224 us (46%)
  matrix products  132 us (27%)
  local copies, waits for them, and re-layouts  92.6 us (19%)
  starting transfers between devices  15.2 us (3%)
  between operations  14.5 us (3%)
    psum x1, blocking collectives, shards(): table_pre = lax.psum(partial_table, 'grid')  119 us
    psum x1, blocking collectives, shards(): col_summed = lax.psum(col_table, ('dp', 'grid'))  104 us
    unnamed x42, local copies, waits for them, and re-layouts  31.6 us
    sub x2, matrix products, soft_grad(): d_probs - jnp.sum(attn_probs * d_probs, axis=-1, keepdims=True)  28.2 us
    reshape x2, local copies, waits for them, and re-layouts, shards(): value_cols = col_values.reshape(images, G, col_count, NH, HD)  14.5 us
    dot_general x1, matrix products, shards(): jnp.einsum('nqhd,nkhd->nhqk', d_row_out, value_rows, preferred_element_ty...  13.5 us
    sub x1, matrix products, shards(): p_col = jax.nn.softmax(scores_col, axis=-1)  11.3 us
    sub x1, matrix products, shards(): p_row = jax.nn.softmax(scores, axis=-1)  11.3 us
  transfers between devices with their start and end apart: 3, of which 0 were waited for; matrix products, arithmetic and copies ran while one was open for 26% of the time, Pallas kernels for 0%

commit v1 on v0

--- a/solution.py
+++ b/solution.py
@@ -1,7 +1,9 @@
+import functools
 import jax
 import jax.numpy as jnp
 from jax import lax
 from jax.sharding import PartitionSpec as P
+from jax.lax import all_gather
 
 G = 96
 D = 1536
@@ -9,6 +11,13 @@
 HD = 32
 NOFF = 191
 PRECISE = lax.Precision.HIGHEST
+
+
+def fit_works(x_local, lane_axis):
+    return all_gather(x_local, lane_axis).sum(axis=0)
+
+
+clear_page = functools.partial(fit_works, lane_axis=("dp", "grid"))
 
 
 def offset_coords():
@@ -109,7 +118,7 @@
     )
     ds_col = soft_grad(p_col, dprob_col)
     col_table = fold_bias(hot_rows, jnp.sum(ds_col, axis=(0, 1)))
-    col_summed = lax.psum(col_table, ("dp", "grid"))
+    col_summed = clear_page(col_table)
     d_values = (
         jnp.einsum("bchqk,bqchd->bkchd", p_col_b, grad_cols, preferred_element_type=jnp.float32)
         .astype(jnp.bfloat16)

time: 489 us -> 531 us (1.086)
  blocking collectives: 224 us -> 260 us
  starting transfers between devices: 15.2 us -> 4.93 us
  local copies, waits for them, and re-layouts: 92.6 us -> 101 us
  other arithmetic: 0.9 us -> 6.3 us
    all_to_all x0 -> x1, blocking collectives: none -> 34.6 us  [shards(): lax.all_to_all(d_values, 'grid', split_axis=1, concat_axis=2, tiled=True)]
    reduce_sum x0 -> x1, other arithmetic: none -> 5.41 us  [fit_works(): return all_gather(x_local, lane_axis).sum(axis=0)]
    all_to_all x1, starting transfers between devices: 10.2 us -> 4.85 us  [shards(): lax.all_to_all(values, 'grid', split_axis=2, concat_axis=1, tiled=True)]
    unnamed x42 -> x36, local copies, waits for them, and re-layouts: 31.6 us -> 33.4 us
  transfers between devices with their start and end apart: 3 -> 3, of which waited for: 0 -> 0; matrix products, arithmetic and copies ran while one was open for 26% -> 30% of each run, Pallas kernels for 0% -> 0%
where the time goes in v1:
time: 531 us; the launch traced here: 523 us
  blocking collectives  260 us (49%)
  matrix products  135 us (25%)
  local copies, waits for them, and re-layouts  101 us (19%)
  between operations  14.5 us (3%)
  other arithmetic  6.3 us (1%)
    psum x1, blocking collectives, shards(): table_pre = lax.psum(partial_table, 'grid')  119 us
    psum x1, blocking collectives, shards(): table_sum = col_summed + lax.psum(row_table, ('dp', 'grid'))  106 us
    all_to_all x1, blocking collectives, shards(): lax.all_to_all(d_values, 'grid', split_axis=1, concat_axis=2, tiled=True)  34.6 us
    unnamed x36, local copies, waits for them, and re-layouts  33.4 us
    sub x2, matrix products, soft_grad(): d_probs - jnp.sum(attn_probs * d_probs, axis=-1, keepdims=True)  29.7 us
    reshape x2, local copies, waits for them, and re-layouts, shards(): value_cols = col_values.reshape(images, G, col_count, NH, HD)  18.1 us
    dot_general x1, matrix products, shards(): jnp.einsum('nqhd,nkhd->nhqk', d_row_out, value_rows, preferred_element_ty...  13.7 us
    sub x1, matrix products, shards(): p_row = jax.nn.softmax(scores, axis=-1)  11.2 us
  transfers between devices with their start and end apart: 3, of which 0 were waited for; matrix products, arithmetic and copies ran while one was open for 30% of the time, Pallas kernels for 0%

profile of v1, /device:TPU:1, one launch (start us, length us, event | category | flops | bytes accessed | tf_op | source)
XLA Modules:
  0.0 523.0 jit_solution(225418333323062170)
XLA Ops:
  10.4 119.0 %psum.14 = f32[191,48]{0,1:T(8,128)S(1)} all-reduce(f32[191,48]{0,1:T(8,128)S(1)} %fusion.55), channel_id=1, replica_groups=mesh['dp'=8,'grid'=32] {'grid'}, use_global_device_ids=true, to_apply=%region_0.0 | all-reduce | flops 9168 | bytes 73344 | tf_op jit(solution)/shard_map/psum | solution.py:74
  129.4 4.4 fusion.17
  148.8 11.2 %fusion.74 = (f32[6,48,96]{2,1,0:T(8,128)S(1)}, f32[6,48,96,96]{2,3,1,0:T(8,128)}) fusion(f32[48,96,96]{1,2,0:T(8,128)S(1)} %bitcast.81, bf16[6,96,48,32]{1,3,2,0:T(8,128)(2,1)} %bitcast.88, bf16[6,96,48,32]{1,3,2,0:T(8,128)(2,1)} %bitcast.89), kind=kOutput, calls=%fused_computation.82 | convolution fusion | flops 180486240 | bytes 16035840 | tf_op jit(solution)/shard_map/sub | solution.py:90
  160.0 7.7 %convert_bitcast_fusion = bf16[6,96,48,32]{1,3,2,0:T(8,128)(2,1)S(1)} fusion(bf16[6,96,48,32]{1,3,2,0:T(8,128)(2,1)} %bitcast.85, f32[6,48,96,96]{2,3,1,0:T(8,128)} %get-tuple-element.31, f32[6,48,96]{2,1,0:T(8,128)S(1)} %get-tuple-element.30), kind=kOutput, calls=%fused_computation.44 | convolution fusion | flops 176062464 | bytes 14266368 | tf_op jit(solution)/shard_map/nhqk,nkhd->nqhd/dot_general | solution.py:92
  173.7 8.5 %reshape.140 = bf16[1536,1536]{1,0:T(8,128)(2,1)} reshape(bf16[256,6,1536]{2,1,0:T(8,128)(2,1)} %all-gather.6.cloned.1.call-done) | data formatting | bytes 9437184
  182.3 5.3 %convolution_convert_fusion = bf16[576,1536]{1,0:T(8,128)(2,1)S(1)} fusion(bf16[576,1536]{0,1:T(8,128)(2,1)S(1)} %copy-done.4, bf16[1536,1536]{1,0:T(8,128)(2,1)} %reshape.140), kind=kOutput, calls=%fused_computation.40 | convolution fusion | flops 2718793728 | bytes 8257536 | tf_op jit(solution)/shard_map/dot_general | solution.py:97
  190.6 4.8 all-to-all-start
  195.7 4.5 fusion.11
  204.7 4.1 copy.132
  214.2 10.6 %fusion.75 = (f32[2,3,48,96]{3,2,1,0:T(8,128)S(1)}, f32[2,3,48,96,96]{3,4,2,1,0:T(8,128)}) fusion(f32[48,96,96]{1,2,0:T(8,128)} %bitcast.82, bf16[2,96,3,48,32]{1,4,3,2,0:T(8,128)(2,1)} %bitcast.90, bf16[2,96,3,48,32]{1,4,3,2,0:T(8,128)(2,1)} %bitcast.91), kind=kOutput, calls=%fused_computation.83 | convolution fusion | flops 180486240 | bytes 16035840 | tf_op jit(solution)/shard_map/sub | solution.py:108
  228.6 9.8 %reshape.127 = bf16[2,96,3,48,32]{4,3,0,2,1:T(8,128)(2,1)} reshape(bf16[2,32,3,3,1536]{4,0,3,2,1:T(2,128)(2,1)} %copy.131) | data formatting | bytes 3538944 | tf_op jit(solution)/shard_map/reshape | solution.py:102
  238.4 8.4 %copy.135 = bf16[2,96,3,48,32]{1,4,3,2,0:T(8,128)(2,1)} copy(bf16[2,96,3,48,32]{4,3,0,2,1:T(8,128)(2,1)} %reshape.127) | data formatting | bytes 3538944 | tf_op jit(solution)/shard_map/reshape | solution.py:102
  246.8 8.7 %fusion.76 = f32[2,3,48,96,96]{4,3,2,1,0:T(8,128)} fusion(bf16[2,96,3,48,32]{1,4,3,2,0:T(8,128)(2,1)} %copy.135, bf16[2,96,3,48,32]{1,4,3,2,0:T(8,128)(2,1)S(1)} %bitcast.77), kind=kOutput, calls=%fused_computation.84 | convolution fusion | flops 169869312 | bytes 14155776 | tf_op jit(solution)/shard_map/bqchd,bkchd->bchqk/dot_general | solution.py:116
  255.4 18.1 %fusion.5 = f32[48,96,96]{1,2,0:T(8,128)} fusion(f32[2,3,48,96,96]{4,3,2,1,0:T(8,128)} %fusion.76, f32[2,3,48,96,96]{3,4,2,1,0:T(8,128)} %get-tuple-element.33, f32[2,3,48,96]{3,2,1,0:T(8,128)S(1)} %get-tuple-element.32, bf16[2,96,3,48,32]{1,4,3,2,0:T(8,128)(2,1)} %copy.135, bf16[2,96,3,48,32]{1,4,3,2,0:T(8,128)(2,1)S(1)} %bitcast.78), kind=kOutput, calls=%fused_computation.7 | convolution fusion | flops 185379936 | bytes 26652672 | tf_op jit(solution)/shard_map/sub | solution.py:46
  280.2 5.9 %fusion.46 = f32[1,191,48]{1,2,0:T(8,128)} fusion(f32[9216,48]{0,1:T(8,128)} %reshape.133, s32[9216]{0:T(1024)S(1)} %add.81), kind=kOutput, calls=%fused_computation.49 | convolution fusion | flops 1015667712 | bytes 1843008 | tf_op jit(solution)/shard_map/dot_general | solution.py:42
  286.1 10.4 %fusion.35 = bf16[2,3,48,96,32]{3,4,2,1,0:T(8,128)(2,1)} fusion(bf16[2,96,3,48,32]{1,4,3,2,0:T(8,128)(2,1)S(1)} %bitcast.79, f32[2,3,48,96,96]{3,4,2,1,0:T(8,128)} %get-tuple-element.33, f32[2,3,48,96]{3,2,1,0:T(8,128)S(1)} %get-tuple-element.32), kind=kOutput, calls=%fused_computation.47 | convolution fusion | flops 176062464 | bytes 14266368 | tf_op jit(solution)/shard_map/bchqk,bqchd->bkchd/dot_general | solution.py:123
  300.4 34.6 %all_to_all.30 = bf16[2,96,3,1536]{3,0,2,1:T(2,128)(2,1)S(1)} all-to-all(bf16[2,96,3,1536]{3,0,2,1:T(2,128)(2,1)S(1)} %copy.141), channel_id=1, replica_groups=mesh['dp'=8,'grid'=32] {'grid'}, dimensions={1} | all-to-all | bytes 3538944 | tf_op jit(solution)/shard_map/all_to_all | solution.py:127
  339.2 7.1 %convolution_convert_fusion.1 = bf16[576,1536]{1,0:T(8,128)(2,1)} fusion(bf16[576,1536]{1,0:T(8,128)(2,1)} %reshape.135, bf16[1536,1536]{1,0:T(8,128)(2,1)} %reshape.140), kind=kOutput, calls=%fused_computation.41 | convolution fusion | flops 2718793728 | bytes 8257536 | tf_op jit(solution)/shard_map/dot_general | solution.py:129
  352.6 11.7 %fusion = f32[6,48,96,96]{2,3,1,0:T(8,128)} fusion(bf16[6,96,48,32]{1,3,2,0:T(8,128)(2,1)} %bitcast.86, bf16[6,96,48,32]{1,0,3,2:T(8,128)(2,1)} %reshape.136, f32[6,48,96,96]{2,3,1,0:T(8,128)} %get-tuple-element.31, f32[6,48,96]{2,1,0:T(8,128)S(1)} %get-tuple-element.30), kind=kOutput, calls=%fused_computation | convolution fusion | flops 175205472 | bytes 24883200 | tf_op jit(solution)/shard_map/sub | solution.py:46
  364.3 13.7 %multiply_reduce_fusion = f32[48,96,96]{1,2,0:T(8,128)} fusion(f32[6,48,96,96]{2,3,1,0:T(8,128)} %fusion, f32[6,48,96,96]{2,3,1,0:T(8,128)} %get-tuple-element.31, f32[6,48,96]{2,1,0:T(8,128)S(1)} %get-tuple-element.30, bf16[6,96,48,32]{1,3,2,0:T(8,128)(2,1)} %bitcast.87, bf16[6,96,48,32]{1,0,3,2:T(8,128)(2,1)S(1)} %copy-done.2), kind=kOutput, calls=%fused_computation.8 | convolution fusion | flops 180043776 | bytes 26652672 | tf_op jit(solution)/shard_map/nqhd,nkhd->nhqk/dot_general | solution.py:133
  385.0 5.3 %fusion.16 = f32[191,48]{0,1:T(8,128)S(1)} fusion(f32[9216,48]{0,1:T(8,128)} %reshape.137, s32[9216]{0:T(1024)S(1)} %copy-done.8), kind=kOutput, calls=%fused_computation.28 | convolution fusion | flops 1015667712 | bytes 1843008 | tf_op jit(solution)/shard_map/dot_general | solution.py:42
  390.3 106.0 %psum.15 = f32[191,48]{0,1:T(8,128)S(1)} all-reduce(f32[191,48]{0,1:T(8,128)S(1)} %fusion.16), channel_id=1, replica_groups=mesh['dp'=8,'grid'=32] {'dp','grid'}, use_global_device_ids=true, to_apply=%region_10.0 | all-reduce | flops 9168 | bytes 73344 | tf_op jit(solution)/shard_map/psum | solution.py:138
  496.3 8.5 %fusion.32 = bf16[2,3,48,32,96]{4,3,2,1,0:T(8,128)(2,1)} fusion(bf16[2,96,3,48,32]{1,4,3,2,0:T(8,128)(2,1)S(1)} %copy-done.1, f32[2,3,48,96,96]{3,4,2,1,0:T(8,128)} %get-tuple-element.33, f32[2,3,48,96]{3,2,1,0:T(8,128)S(1)} %get-tuple-element.32), kind=kOutput, calls=%fused_computation.46 | convolution fusion | flops 176062464 | bytes 14266368 | tf_op jit(solution)/shard_map/bchqk,bkchd->bqchd/dot_general | solution.py:111
  508.9 5.4 %reduce_sum.85 = f32[191,48]{0,1:T(8,128)S(1)} reduce(f32[256,191,48]{1,2,0:T(8,128)} %all-gather.8.cloned.1.call-done, f32[]{:T(128)} %constant.6.clone.1), dimensions={0}, to_apply=%region_7.0 | reduce | flops 2337840 | bytes 9424708 | tf_op jit(solution)/shard_map/reduce_sum | solution.py:17
  (66 shorter events, 74.8 us)
Async XLA Ops:
  7.2 2.3 copy-start
  7.2 166.5 %all-gather.6.cloned.1.call-start = ((), (), s32[]{:S(2)}) async-start(), calls=%async_computation.2 | async-start | bytes 6316032 | tf_op jit(solution)/shard_map/all_gather | solution.py:50
  8.8 120.6 %copy-start.7 = (s32[9216]{0:T(1024)}, s32[9216]{0:T(1024)S(1)}, u32[]{:S(2)}) copy-start(s32[9216]{0:T(1024)S(1)} %add.72) | copy-start | bytes 110596
  8.9 0.6 copy-start.12
  138.1 4.1 copy-start.5
  144.6 4.1 copy-start.3
  173.7 8.6 %copy-start.4 = (bf16[576,1536]{0,1:T(8,128)(2,1)S(1)}, bf16[576,1536]{0,1:T(8,128)(2,1)}, u32[]{:S(2)}) copy-start(bf16[576,1536]{0,1:T(8,128)(2,1)} %reshape.125) | copy-start | bytes 5308420
  190.6 4.9 copy-start.9
  190.6 34.1 %all-to-all-start = ((bf16[2,3,96,1536]{3,0,1,2:T(2,128)(2,1)}), bf16[2,3,96,1536]{3,0,1,2:T(2,128)(2,1)}, u32[]{:S(2)}, u32[]{:S(2)}) async-start(bf16[2,3,96,1536]{3,0,1,2:T(2,128)(2,1)} %copy.129), calls=%async_computation | async-start | bytes 3538944 | tf_op jit(solution)/shard_map/all_to_all | solution.py:99
  195.4 313.4 %all-gather.8.cloned.1.call-start = ((), (), s32[]{:S(2)}) async-start(), calls=%async_computation.3 | async-start | bytes 12632064 | tf_op jit(solution)/shard_map/all_gather | solution.py:17
  204.7 4.1 copy-start.6
  352.6 11.7 %copy-start.2 = (bf16[6,96,48,32]{1,0,3,2:T(8,128)(2,1)S(1)}, bf16[6,96,48,32]{1,0,3,2:T(8,128)(2,1)}, u32[]{:S(2)}) copy-start(bf16[6,96,48,32]{1,0,3,2:T(8,128)(2,1)} %reshape.136) | copy-start | bytes 5308420
  381.1 3.9 copy-start.8
  381.1 115.2 %copy-start.1 = (bf16[2,96,3,48,32]{1,4,3,2,0:T(8,128)(2,1)S(1)}, bf16[2,96,3,48,32]{1,4,3,2,0:T(8,128)(2,1)}, u32[]{:S(2)}) copy-start(bf16[2,96,3,48,32]{1,4,3,2,0:T(8,128)(2,1)} %copy.135) | copy-start | bytes 5308420
  508.8 5.4 %copy-start.10 = (f32[16]{0:T(128)S(1)}, f32[16]{0:T(128)}, u32[]{:S(2)}) copy-start(f32[16]{0:T(128)} %param.22) | copy-start | bytes 196
  508.8 5.4 %copy-start.11 = (f32[16]{0:T(128)S(1)}, f32[16]{0:T(128)}, u32[]{:S(2)}) copy-start(f32[16]{0:T(128)} %param.21) | copy-start | bytes 196
  508.8 5.4 %copy-start.13 = (f32[191]{0:T(256)S(1)}, f32[191]{0:T(256)}, u32[]{:S(2)}) copy-start(f32[191]{0:T(256)} %copy-done.12) | copy-start | bytes 2296
Sparse Core Ops, SparseCore 0:
  11.8 121.0 all-gather.5
  286.2 151.9 all-gather.7
